TPU v7x, 32 devices: a whole 2x2x4 slice. The times are simulated.
32 devices in a mesh: dp: 8 (over y, x, core), tp: 4 (over z).
Axes of the slice: x: 2, y: 2, z: 4, core: 2. Of those that a mesh axis runs over, the one named last changes fastest.
Arguments:
- block_in: bfloat16 [128, 4, 37632], P('dp', 'tp'), may hold values from -6 to 6
- ln1_gain: float32 [768], P('tp'), may hold values from 0.1 to 1.9
- ln1_shift: float32 [768], P('tp'), may hold values from -1.75 to 1.75
- tok_w1: float32 [196, 384], replicated, may hold values from -0.4375 to 0.4375
- tok_b1: float32 [384], replicated, may hold values from -1.75 to 1.75
- tok_w2: float32 [384, 196], replicated, may hold values from -0.3125 to 0.3125
- tok_b2: float32 [196], replicated, may hold values from -1.75 to 1.75
- ln2_gain: float32 [768], P('tp'), may hold values from 0.1 to 1.9
- ln2_shift: float32 [768], P('tp'), may hold values from -1.75 to 1.75
- ch_w1: float32 [768, 3072], P('dp', 'tp'), may hold values from -0.21875 to 0.21875
- ch_b1: float32 [3072], replicated, may hold values from -1.75 to 1.75
- ch_w2: float32 [3072, 768], P('tp', 'dp'), may hold values from -0.109375 to 0.109375
- ch_b2: float32 [768], replicated, may hold values from -1.75 to 1.75
- group_ids: int32 [128], P('dp'), may hold values from 0 to 63
- out_grad: bfloat16 [128, 4, 37632], P('dp', 'tp'), may hold values from -6 to 6
Outputs:
- block_out: bfloat16 [128, 4, 37632], P('dp', 'tp')
- dx: bfloat16 [128, 4, 37632], P('dp', 'tp')
- group_norms: float32 [64], replicated
- d_ln1_gain: float32 [768], P('tp')
- d_ln1_shift: float32 [768], P('tp')
- d_tok_w1: float32 [196, 384], replicated
- d_tok_b1: float32 [384], replicated
- d_tok_w2: float32 [384, 196], replicated
- d_tok_b2: float32 [196], replicated
- d_ln2_gain: float32 [768], P('tp')
- d_ln2_shift: float32 [768], P('tp')
- d_ch_w1: float32 [768, 3072], P('dp', 'tp')
- d_ch_b1: float32 [3072], replicated
- d_ch_w2: float32 [3072, 768], P('tp', 'dp')
- d_ch_b2: float32 [768], replicated
All inputs are finite; a program needn't handle non-finite values.
Results may differ from a plain program's by a relative error of at most 0.01.
Values may be sent and summed in bfloat16 or wider, within the bound.
A program may use at most 128 MiB of HBM per device.

v0:
```python
import math
import jax
import jax.numpy as jnp
from jax import lax
from jax.sharding import PartitionSpec as P

S = 196
GROUPS = 64
epsilon = 1e-06
highest = lax.Precision.HIGHEST


def in_blocks(array, dim, size):
    lengths = array.shape
    tiles = array.reshape(*lengths[:dim], size, lengths[dim] // size, *lengths[dim + 1 :])
    return jnp.moveaxis(tiles, dim, 0)


def sum_at_owner(array, axis, dim):
    size = lax.axis_size(axis)
    tiles = lax.all_to_all(in_blocks(array, dim, size), axis, 0, 0, tiled=True)
    return jnp.sum(tiles.astype(jnp.float32), axis=0)


def norm_stats(values, full_width):
    totals = lax.psum((jnp.sum(values, -1), jnp.sum(values * values, -1)), "tp")
    average = totals[0] / full_width
    inverse = lax.rsqrt(totals[1] / full_width - average * average + epsilon)
    return ((values - average[..., None]) * inverse[..., None], inverse)


def norm_back(grad_hat, normed, inverse, full_width):
    totals = lax.psum((jnp.sum(grad_hat, -1), jnp.sum(grad_hat * normed, -1)), "tp")
    return inverse[..., None] * (
        grad_hat - totals[0][..., None] / full_width - normed * totals[1][..., None] / full_width
    )


def spread_slot(values, slot_mask):
    expanded = values[..., None, :] * slot_mask[:, None]
    return expanded.reshape(values.shape[:-1] + (slot_mask.shape[0] * values.shape[-1],))


def gather_channels(values):
    return lax.all_gather(values, "tp", axis=1, tiled=True)


def sum_channels(values):
    return lax.psum_scatter(
        values.astype(jnp.bfloat16), "tp", scatter_dimension=1, tiled=True
    ).astype(jnp.float32)


def per_device(
    block_in,
    ln1_gain,
    ln1_shift,
    tok_w1,
    tok_b1,
    tok_w2,
    tok_b2,
    ln2_gain,
    ln2_shift,
    ch_w1,
    ch_b1,
    ch_w2,
    ch_b2,
    group_ids,
    out_grad,
):
    f32 = jnp.float32
    bf16 = jnp.bfloat16
    images = block_in.shape[0]
    patches = S
    plain_in = block_in.reshape(images, patches, -1)
    plain_grad = out_grad.reshape(images, patches, -1)
    local_width = plain_in.shape[2]
    tp_count = lax.axis_size("tp")
    dp_count = lax.axis_size("dp")
    tp_place = lax.axis_index("tp")
    full_width = local_width * tp_count
    slot_mask = (jnp.arange(tp_count) == tp_place).astype(f32)
    row_count = images * patches
    input_float = plain_in.astype(f32)
    normed_one, inverse_one = norm_stats(input_float, full_width)
    mixed_in = (normed_one * ln1_gain + ln1_shift).astype(bf16)
    token_w1 = tok_w1.astype(bf16)
    token_w2 = tok_w2.astype(bf16)
    pre_act = jnp.einsum("nsc,sk->nck", mixed_in, token_w1, preferred_element_type=f32) + tok_b1
    hidden_act, gelu_token = jax.vjp(jax.nn.gelu, pre_act)
    hidden_low = hidden_act.astype(bf16)
    token_out = (
        jnp.einsum("nck,ks->nsc", hidden_low, token_w2, preferred_element_type=f32)
        + tok_b2[None, :, None]
    )
    residual = input_float + token_out
    normed_two, inverse_two = norm_stats(residual, full_width)
    branch_in = (normed_two * ln2_gain + ln2_shift).astype(bf16).reshape(row_count, local_width)
    grad_low = plain_grad.reshape(row_count, local_width)
    upper_rows, lower_rows = (
        lax.all_gather(ch_w1.astype(bf16), "dp", axis=0, tiled=True),
        lax.all_gather(ch_w2.astype(bf16), "dp", axis=1, tiled=True),
    )
    gathered = gather_channels(branch_in)
    hidden_width = upper_rows.shape[1]
    bias_first = lax.dynamic_slice_in_dim(ch_b1, tp_place * hidden_width, hidden_width)
    bias_second = lax.dynamic_slice_in_dim(ch_b2, tp_place * local_width, local_width)
    inner_act = jnp.dot(gathered, upper_rows, preferred_element_type=f32) + bias_first
    activated, gelu_branch = jax.vjp(jax.nn.gelu, inner_act)
    activated_low = activated.astype(bf16)
    branch_sum = (
        sum_channels(jnp.dot(activated_low, lower_rows, preferred_element_type=f32)) + bias_second
    )
    branch_low = branch_sum.astype(bf16)
    grad_full = gather_channels(grad_low)
    grad_activated = jnp.dot(grad_full, lower_rows.T, preferred_element_type=f32)
    grad_lower = jnp.dot(activated_low.T, grad_full, preferred_element_type=f32)
    grad_inner = gelu_branch(grad_activated)[0].astype(bf16)
    grad_upper = jnp.dot(gathered.T, grad_inner, preferred_element_type=f32)
    bias_first_grad = spread_slot(jnp.sum(grad_inner.astype(f32), 0), slot_mask)
    bias_second_grad = spread_slot(jnp.sum(grad_low.astype(f32), 0), slot_mask)
    grad_branch = sum_channels(jnp.dot(grad_inner, upper_rows.T, preferred_element_type=f32))
    upper_grad, lower_grad = (
        sum_at_owner(grad_upper.astype(jnp.bfloat16), "dp", 0),
        sum_at_owner(grad_lower.astype(jnp.bfloat16), "dp", 1),
    )
    output = (residual + branch_low.astype(f32).reshape(residual.shape)).astype(bf16)
    grad_normed = grad_branch.reshape(residual.shape)
    image_gain = jnp.sum(grad_normed * normed_two, 1)
    image_shift = jnp.sum(grad_normed, 1)
    grad_resid = plain_grad.astype(f32) + norm_back(
        grad_normed * ln2_gain, normed_two, inverse_two, full_width
    )
    grad_token_low = grad_resid.astype(bf16)
    grad_hidden = jnp.einsum("nsc,ks->nck", grad_token_low, token_w2, preferred_element_type=f32)
    token_w2_grad = jnp.einsum(
        "nck,nsc->ks", hidden_low, grad_token_low, preferred_element_type=f32
    )
    token_b2_grad = jnp.sum(grad_token_low.astype(f32), (0, 2))
    grad_pre = gelu_token(grad_hidden)[0].astype(bf16)
    token_w1_grad = jnp.einsum("nsc,nck->sk", mixed_in, grad_pre, preferred_element_type=f32)
    token_b1_grad = jnp.sum(grad_pre.astype(f32), (0, 1))
    grad_mixed = jnp.einsum("nck,sk->nsc", grad_pre, token_w1, preferred_element_type=f32)
    gain_one_grad = jnp.sum(grad_mixed * normed_one, (0, 1))
    shift_one_grad = jnp.sum(grad_mixed, (0, 1))
    grad_input = (
        grad_resid + norm_back(grad_mixed * ln1_gain, normed_one, inverse_one, full_width)
    ).astype(bf16)
    member = (group_ids[:, None] == jnp.arange(GROUPS)[None, :]).astype(f32)
    image_stats = jnp.stack([image_gain, image_shift], 1).reshape(images, 2 * local_width)
    group_local = jnp.dot(member.T, image_stats, precision=highest).reshape(GROUPS, 2, local_width)
    norm_one_local = jnp.stack([gain_one_grad, shift_one_grad], 0)
    totals = lax.psum(
        (
            token_w1_grad,
            token_b1_grad,
            token_w2_grad,
            token_b2_grad,
            spread_slot(group_local, slot_mask),
            spread_slot(norm_one_local, slot_mask),
            bias_first_grad,
            bias_second_grad,
        ),
        ("dp", "tp"),
    )
    group_full = totals[4]
    group_norms = jnp.sqrt(jnp.sum(group_full * group_full, (1, 2)))
    clip_bound = 2.0 * math.sqrt(images * dp_count * patches * full_width / GROUPS)
    factor = clip_bound / jnp.maximum(group_norms, clip_bound)
    clipped = jnp.sum(factor[:, None, None] * group_full, 0)
    clipped_local = lax.dynamic_slice_in_dim(clipped, tp_place * local_width, local_width, 1)
    norm_one_own = lax.dynamic_slice_in_dim(totals[5], tp_place * local_width, local_width, 1)
    stored_out = output.reshape(images, 1, patches * local_width)
    stored_grad = grad_input.reshape(images, 1, patches * local_width)
    return (
        stored_out,
        stored_grad,
        group_norms,
        norm_one_own[0],
        norm_one_own[1],
        totals[0],
        totals[1],
        totals[2],
        totals[3],
        clipped_local[0],
        clipped_local[1],
        upper_grad,
        totals[6],
        lower_grad,
        totals[7],
    )


def solution(mesh):
    in_specs = (
        P("dp", "tp", None),
        P("tp"),
        P("tp"),
        P(),
        P(),
        P(),
        P(),
        P("tp"),
        P("tp"),
        P("dp", "tp"),
        P(),
        P("tp", "dp"),
        P(),
        P("dp"),
        P("dp", "tp", None),
    )
    out_specs = (
        P("dp", "tp", None),
        P("dp", "tp", None),
        P(),
        P("tp"),
        P("tp"),
        P(),
        P(),
        P(),
        P(),
        P("tp"),
        P("tp"),
        P("dp", "tp"),
        P(),
        P("tp", "dp"),
        P(),
    )
    return jax.shard_map(
        per_device, mesh=mesh, in_specs=in_specs, out_specs=out_specs, check_vma=False
    )
```

profile of v0, /device:TPU:0, one launch (start us, length us, event | category | flops | bytes accessed | tf_op | source)
XLA Modules:
  0.0 688.9 jit_solution(15931302584527314932)
XLA Ops:
  15.6 20.9 %all-reduce.5 = (f32[16,196]{1,0:T(8,128)S(1)}, f32[16,196]{1,0:T(8,128)S(1)}) all-reduce(f32[16,196]{1,0:T(8,128)S(1)} %get-tuple-element.20, f32[16,196]{1,0:T(8,128)S(1)} %get-tuple-element.19), channel_id=1, replica_groups=mesh['dp'=8,'tp'=4] {'tp'}, use_global_device_ids=true, to_apply=%region_3.0 | all-reduce | flops 6272 | bytes 50176 | tf_op jit(solution)/shard_map/psum | solution.py:26
  44.6 15.8 %all-reduce.4 = (f32[16,196]{1,0:T(8,128)S(1)}, f32[16,196]{1,0:T(8,128)S(1)}) all-reduce(f32[16,196]{1,0:T(8,128)S(1)} %get-tuple-element.23, f32[16,196]{1,0:T(8,128)S(1)} %get-tuple-element.22), channel_id=1, replica_groups=mesh['dp'=8,'tp'=4] {'tp'}, use_global_device_ids=true, to_apply=%region_7.0 | all-reduce | flops 6272 | bytes 50176 | tf_op jit(solution)/shard_map/psum | solution.py:26
  76.0 84.4 %all-gather.5.cloned.1.call-done = bf16[3136,768]{0,1:T(8,128)(2,1)} async-done(((bf16[3136,192]{0,1:T(8,128)(2,1)}), bf16[3136,768]{0,1:T(8,128)(2,1)}) %all-gather.5.cloned.1.call-update) | async-done | bytes 4816912 | tf_op jit(solution)/shard_map/all_gather | solution.py:45
  160.4 10.4 %fusion.40 = f32[3136,768]{1,0:T(8,128)} fusion(bf16[3136,768]{0,1:T(8,128)(2,1)} %all-gather.5.cloned.1.call-done, bf16[768,768]{1,0:T(8,128)(2,1)} %all-gather.7.cloned.1.call-done), kind=kOutput, calls=%fused_computation.92 | convolution fusion | flops 3699376128 | bytes 15630336 | tf_op jit(solution)/shard_map/dot_general | solution.py:108
  170.8 14.6 %all-gather.9.cloned.1.call-done = bf16[768,768]{0,1:T(8,128)(2,1)} async-done(((bf16[768,96]{0,1:T(8,128)(2,1)}), bf16[768,768]{0,1:T(8,128)(2,1)}) %all-gather.9.cloned.1.call-update) | async-done | bytes 1179664 | tf_op jit(solution)/shard_map/all_gather | solution.py:102
  185.4 10.6 %convolution_convert_fusion.1 = bf16[3136,768]{0,1:T(8,128)(2,1)} fusion(bf16[768,768]{0,1:T(8,128)(2,1)} %all-gather.9.cloned.1.call-done, f32[3136,768]{1,0:T(8,128)} %fusion.40, f32[768]{0:T(1024)S(1)} %dynamic_slice.12), kind=kOutput, calls=%fused_computation.14 | convolution fusion | flops 3725869056 | bytes 15633408 | tf_op jit(solution)/shard_map/dot_general | solution.py:112
  196.4 83.0 %all-gather.11.cloned.1.call-done = bf16[3136,768]{0,1:T(8,128)(2,1)} async-done(((bf16[3136,192]{0,1:T(8,128)(2,1)}), bf16[3136,768]{0,1:T(8,128)(2,1)}) %all-gather.11.cloned.1.call-update) | async-done | bytes 4816912 | tf_op jit(solution)/shard_map/all_gather | solution.py:45
  279.5 15.2 %convert_reduce_fusion = (f32[768]{0:T(1024)S(1)}, bf16[3136,768]{1,0:T(8,128)(2,1)S(1)}) fusion(f32[3136,768]{1,0:T(8,128)} %fusion.40, f32[768]{0:T(1024)S(1)} %dynamic_slice.12, bf16[3136,768]{0,1:T(8,128)(2,1)} %all-gather.11.cloned.1.call-done, bf16[768,768]{0,1:T(8,128)(2,1)} %all-gather.9.cloned.1.call-done), kind=kOutput, calls=%fused_computation.9 | convolution fusion | flops 3754769664 | bytes 20453376 | tf_op jit(solution)/shard_map/dot_general | solution.py:116
  296.8 5.9 convolution_convert_fusion
  302.7 10.6 %convolution_convert_fusion.2 = bf16[768,768]{0,1:T(8,128)(2,1)} fusion(bf16[3136,768]{0,1:T(8,128)(2,1)} %all-gather.11.cloned.1.call-done, f32[3136,768]{1,0:T(8,128)} %fusion.40, f32[768]{0:T(1024)S(1)} %dynamic_slice.12), kind=kOutput, calls=%fused_computation.49 | convolution fusion | flops 3724050432 | bytes 15633408 | tf_op jit(solution)/shard_map/dot_general | solution.py:117
  317.8 9.1 %convolution_convert_fusion.3 = bf16[768,768]{1,0:T(8,128)(2,1)} fusion(bf16[3136,768]{0,1:T(8,128)(2,1)} %all-gather.5.cloned.1.call-done, bf16[3136,768]{1,0:T(8,128)(2,1)} %copy-done.29), kind=kOutput, calls=%fused_computation.50 | convolution fusion | flops 3699965952 | bytes 10813440 | tf_op jit(solution)/shard_map/dot_general | solution.py:119
  326.9 7.7 %all-to-all-done.1 = bf16[8,768,96]{1,2,0:T(8,128)(2,1)} async-done(((bf16[8,768,96]{1,2,0:T(8,128)(2,1)}), bf16[8,768,96]{1,2,0:T(8,128)(2,1)}, u32[]{:S(2)}, u32[]{:S(2)}) %all-to-all-start.1) | async-done | bytes 1179680 | tf_op jit(solution)/shard_map/all_to_all | solution.py:21
  341.9 4.8 copy.76
  357.9 10.7 %reduce-scatter.3.cloned.1.call-done = bf16[3136,192]{0,1:T(8,128)(2,1)} async-done(((bf16[3136,768]{0,1:T(8,128)(2,1)}), bf16[3136,192]{0,1:T(8,128)(2,1)}) %reduce-scatter.3.cloned.1.call-update) | async-done | bytes 1204240 | tf_op jit(solution)/shard_map/reduce_scatter | solution.py:49
  370.1 5.7 reshape.138
  375.8 84.1 %reduce-scatter.5.cloned.1.call-done = bf16[3136,192]{0,1:T(8,128)(2,1)} async-done(((bf16[3136,768]{0,1:T(8,128)(2,1)}), bf16[3136,192]{0,1:T(8,128)(2,1)}) %reduce-scatter.5.cloned.1.call-update) | async-done | bytes 1204240 | tf_op jit(solution)/shard_map/reduce_scatter | solution.py:49
  462.2 5.7 reshape.130
  472.7 19.7 %all-reduce.3 = (f32[16,196]{1,0:T(8,128)}, f32[16,196]{1,0:T(8,128)}) all-reduce(f32[16,196]{1,0:T(8,128)S(1)} %get-tuple-element.18, f32[16,196]{1,0:T(8,128)} %reduce_sum.187), channel_id=1, replica_groups=mesh['dp'=8,'tp'=4] {'tp'}, use_global_device_ids=true, to_apply=%region_13.0 | all-reduce | flops 6272 | bytes 50176 | tf_op jit(solution)/shard_map/psum | solution.py:33
  493.1 8.6 %convert_reduce_fusion.3 = (f32[196]{0:T(256)}, f32[16,196,192]{1,2,0:T(8,128)S(1)}, bf16[16,196,192]{1,2,0:T(8,128)(2,1)}) fusion(f32[16,196,192]{1,2,0:T(8,128)} %copy.76, f32[16,196]{1,0:T(8,128)} %get-tuple-element.34, f32[16,196,192]{1,2,0:T(8,128)} %copy-done.3, f32[16,196]{1,0:T(8,128)S(1)} %get-tuple-element.47, ...), kind=kLoop, calls=%fused_computation.32 | loop fusion | flops 8429372 | bytes 13298192 | tf_op jit(solution)/shard_map/reduce_sum | solution.py:139
  501.7 6.2 convolution_bitcast_fusion
  528.8 16.1 %all-reduce.2 = (f32[16,196]{1,0:T(8,128)S(1)}, f32[16,196]{1,0:T(8,128)S(1)}) all-reduce(f32[16,196]{1,0:T(8,128)S(1)} %get-tuple-element.16, f32[16,196]{1,0:T(8,128)S(1)} %get-tuple-element.21), channel_id=1, replica_groups=mesh['dp'=8,'tp'=4] {'tp'}, use_global_device_ids=true, to_apply=%region_17.0 | all-reduce | flops 6272 | bytes 50176 | tf_op jit(solution)/shard_map/psum | solution.py:33
  544.9 5.3 add_convert_fusion
  555.6 39.9 %all-reduce = (f32[2,768]{1,0:T(2,128)S(1)}, f32[384]{0:T(512)}, f32[196]{0:T(256)}, f32[3072]{0:T(1024)}, f32[768]{0:T(1024)}) all-reduce(f32[2,768]{1,0:T(2,128)S(1)} %broadcast_multiply_fusion.6, f32[384]{0:T(512)S(1)} %copy-done.19, f32[196]{0:T(256)S(1)} %copy-done.18, ...), channel_id=1, replica_groups=mesh['dp'=8,'tp'=4] {'dp','tp'}, use_global_device_ids=true, to_apply=%region_24.0 | all-reduce | flops 5956 | bytes 47648 | tf_op jit(solution)/shard_map/psum | solution.py:153
  595.5 79.3 %all-reduce.8.cloned.1.call-done = (f32[64,2,768]{2,0,1:T(8,128)}, f32[196,384]{1,0:T(8,128)}, f32[384,196]{0,1:T(8,128)}) async-done(((f32[64,2,768]{2,0,1:T(8,128)}, f32[196,384]{1,0:T(8,128)}, f32[384,196]{0,1:T(8,128)}), (f32[64,2,768]{2,0,1:T(8,128)}, f32[196,384]{1,0:T(8,128)}, f32[384,196]{0,1:T(8,128)})) %all-reduce.8.cloned.1.call-update) | async-done | bytes 995344 | tf_op jit(solution)/shard_map/psum | solution.py:153
  (146 shorter events, 99.7 us)
Async XLA Ops:
  7.2 68.8 %all-gather.7.cloned.1.call-start = ((), (), s32[]{:S(2)}) async-start(), calls=%async_computation.5 | async-start | bytes 1327104 | tf_op jit(solution)/shard_map/all_gather | solution.py:101
  8.9 151.5 %all-gather.5.cloned.1.call-start = ((), (), s32[]{:S(2)}) async-start(), calls=%async_computation.4 | async-start | bytes 6144000 | tf_op jit(solution)/shard_map/all_gather | solution.py:45
  12.3 24.2 %copy-start.15 = (f32[192]{0:T(256)S(1)}, f32[192]{0:T(256)}, u32[]{:S(2)}) copy-start(f32[192]{0:T(256)} %param.16) | copy-start | bytes 2308
  12.3 24.2 %copy-start.20 = (f32[192]{0:T(256)S(1)}, f32[192]{0:T(256)}, u32[]{:S(2)}) copy-start(f32[192]{0:T(256)} %param.17) | copy-start | bytes 2308
  15.6 24.6 %copy-start.10 = (f32[196,384]{1,0:T(8,128)S(1)}, f32[196,384]{1,0:T(8,128)}, u32[]{:S(2)}) copy-start(f32[196,384]{1,0:T(8,128)} %param.18) | copy-start | bytes 903172
  42.1 18.4 %copy-start.13 = (f32[192]{0:T(256)S(1)}, f32[192]{0:T(256)}, u32[]{:S(2)}) copy-start(f32[192]{0:T(256)} %param.22) | copy-start | bytes 2308
  44.6 19.2 %copy-start.3 = (f32[16,196,192]{1,2,0:T(8,128)}, f32[16,196,192]{1,2,0:T(8,128)S(1)}, u32[]{:S(2)}) copy-start(f32[16,196,192]{1,2,0:T(8,128)S(1)} %get-tuple-element.55) | copy-start | bytes 7225348
  68.1 117.2 %all-gather.9.cloned.1.call-start = ((), (), s32[]{:S(2)}) async-start(), calls=%async_computation.6 | async-start | bytes 1327104 | tf_op jit(solution)/shard_map/all_gather | solution.py:102
  69.8 209.6 %all-gather.11.cloned.1.call-start = ((), (), s32[]{:S(2)}) async-start(), calls=%async_computation.8 | async-start | bytes 6144000 | tf_op jit(solution)/shard_map/all_gather | solution.py:45
  74.9 293.6 %reduce-scatter.3.cloned.1.call-start = ((), (), s32[]{:S(2)}) async-start(), calls=%async_computation.7 | async-start | bytes 6144000 | tf_op jit(solution)/shard_map/reduce_scatter | solution.py:49
  196.0 100.9 %copy-start.23 = (bf16[768,768]{1,0:T(8,128)(2,1)S(1)}, bf16[768,768]{1,0:T(8,128)(2,1)}, u32[]{:S(2)}) copy-start(bf16[768,768]{1,0:T(8,128)(2,1)} %all-gather.7.cloned.1.call-done) | copy-start | bytes 3538948
  196.0 263.8 %reduce-scatter.5.cloned.1.call-start = ((), (), s32[]{:S(2)}) async-start(), calls=%async_computation.9 | async-start | bytes 6144000 | tf_op jit(solution)/shard_map/reduce_scatter | solution.py:49
  313.3 21.3 %all-to-all-start.1 = ((bf16[8,768,96]{1,2,0:T(8,128)(2,1)}), bf16[8,768,96]{1,2,0:T(8,128)(2,1)}, u32[]{:S(2)}, u32[]{:S(2)}) async-start(bf16[8,768,96]{1,2,0:T(8,128)(2,1)} %bitcast.18), calls=%async_computation.3 | async-start | bytes 2359296 | tf_op jit(solution)/shard_map/all_to_all | solution.py:21
  326.8 12.1 %copy-start.8 = (bf16[16,1,37632]{2,0,1:T(8,128)(2,1)S(1)}, bf16[16,1,37632]{2,0,1:T(8,128)(2,1)}, u32[]{:S(2)}) copy-start(bf16[16,1,37632]{2,0,1:T(8,128)(2,1)} %param.29) | copy-start | bytes 3612676
  334.6 21.1 %all-to-all-start = ((bf16[8,96,768]{2,1,0:T(8,128)(2,1)}), bf16[8,96,768]{2,1,0:T(8,128)(2,1)}, u32[]{:S(2)}, u32[]{:S(2)}) async-start(bf16[8,96,768]{2,1,0:T(8,128)(2,1)} %bitcast.81), calls=%async_computation.2 | async-start | bytes 2359296 | tf_op jit(solution)/shard_map/all_to_all | solution.py:21
  338.9 335.9 %all-reduce.8.cloned.1.call-start = ((), (), s32[]{:S(2)}) async-start(), calls=%async_computation.10 | async-start | bytes 2015232 | tf_op jit(solution)/shard_map/psum | solution.py:153
  370.0 89.8 %copy-start.14 = (f32[192]{0:T(256)S(1)}, f32[192]{0:T(256)}, u32[]{:S(2)}) copy-start(f32[192]{0:T(256)} %param.22) | copy-start | bytes 2308
  493.1 8.6 %copy-start.27 = (f32[384]{0:T(512)S(1)}, f32[384]{0:T(512)}, u32[]{:S(2)}) copy-start(f32[384]{0:T(512)} %param.19) | copy-start | bytes 4612
  493.1 14.8 %slice-start = ((s8[4718592]{0:T(1024)(128)(4,1)}), s8[4194304]{0:T(1024)(128)(4,1)S(1)}, s32[]{:S(2)}) async-start(s8[4718592]{0:T(1024)(128)(4,1)} %bitcast.79), calls=%async_computation.11 | async-start | bytes 8388608
  501.7 6.2 copy-start.4
  501.7 6.2 slice-start.1
  501.7 6.2 copy-start.25
  523.0 22.0 %copy-start.2 = (f32[16,196,192]{1,2,0:T(8,128)S(1)}, f32[16,196,192]{1,2,0:T(8,128)}, u32[]{:S(2)}) copy-start(f32[16,196,192]{1,2,0:T(8,128)} %copy.70) | copy-start | bytes 7225348
  523.0 22.0 %copy-start.17 = (f32[192]{0:T(256)S(1)}, f32[192]{0:T(256)}, u32[]{:S(2)}) copy-start(f32[192]{0:T(256)} %param.16) | copy-start | bytes 2308
  (17 other events, 51.9 us)
Sparse Core Ops, SparseCore 0:
  10.5 26.7 all-gather.6
  68.2 92.0 all-gather.4
  162.8 22.4 all-gather.8
  186.8 92.6 all-gather.10
  281.6 86.8 reduce-scatter.2
  370.8 88.9 reduce-scatter.4
  545.0 129.7 all-reduce.7
where the time goes:
time: 698 us; the launch traced here: 689 us
  waiting for transfers between devices  369 us (53%)
  blocking collectives  112 us (16%)
  matrix products  81.5 us (12%)
  local copies, waits for them, and re-layouts  59.5 us (9%)
  other arithmetic  42.3 us (6%)
  between operations  15 us (2%)
  starting transfers between devices  9.6 us (1%)
    all_gather x2, waiting for transfers between devices, gather_channels(): return lax.all_gather(values, 'tp', axis=1, tiled=True)  167 us
    reduce_scatter x2, waiting for transfers between devices, sum_channels(): lax.psum_scatter(values.astype(jnp.bfloat16), 'tp', scatter_dimension=1,...  94.7 us
    psum x1, waiting for transfers between devices, per_device(): lax.psum((token_w1_grad, token_b1_grad, token_w2_grad, token_b2_grad, spr...  79.3 us
    psum x1, blocking collectives, per_device(): lax.psum((token_w1_grad, token_b1_grad, token_w2_grad, token_b2_grad, spr...  39.9 us
    psum x2, blocking collectives, norm_stats(): totals = lax.psum((jnp.sum(values, -1), jnp.sum(values * values, -1)), 'tp')  36.8 us
    psum x2, blocking collectives, norm_back(): lax.psum((jnp.sum(grad_hat, -1), jnp.sum(grad_hat * normed, -1)), 'tp')  35.7 us
    dot_general x1, matrix products, per_device(): jnp.dot(grad_full, lower_rows.T, preferred_element_type=f32)  15.2 us
    all_gather x1, waiting for transfers between devices, per_device(): lax.all_gather(ch_w2.astype(bf16), 'dp', axis=1, tiled=True)  14.6 us
  transfers between devices with their start and end apart: 9, of which 8 were waited for; matrix products, arithmetic and copies ran while one was open for 18% of the time, Pallas kernels for 0%

commit v1 on v0

--- a/solution.py
+++ b/solution.py
@@ -150,19 +150,18 @@
     image_stats = jnp.stack([image_gain, image_shift], 1).reshape(images, 2 * local_width)
     group_local = jnp.dot(member.T, image_stats, precision=highest).reshape(GROUPS, 2, local_width)
     norm_one_local = jnp.stack([gain_one_grad, shift_one_grad], 0)
-    totals = lax.psum(
-        (
-            token_w1_grad,
-            token_b1_grad,
-            token_w2_grad,
-            token_b2_grad,
-            spread_slot(group_local, slot_mask),
-            spread_slot(norm_one_local, slot_mask),
-            bias_first_grad,
-            bias_second_grad,
-        ),
-        ("dp", "tp"),
-    )
+    totals = (
+        token_w1_grad,
+        token_b1_grad,
+        token_w2_grad,
+        token_b2_grad,
+        spread_slot(group_local, slot_mask),
+        spread_slot(norm_one_local, slot_mask),
+        bias_first_grad,
+        bias_second_grad,
+    )
+    for over in ("tp", "dp"):
+        totals = lax.psum(totals, over)
     group_full = totals[4]
     group_norms = jnp.sqrt(jnp.sum(group_full * group_full, (1, 2)))
     clip_bound = 2.0 * math.sqrt(images * dp_count * patches * full_width / GROUPS)

time: 698 us -> 662 us (0.948)
  waiting for transfers between devices: 369 us -> 339 us
  blocking collectives: 112 us -> 99.5 us
    psum x1 -> x2, waiting for transfers between devices: 79.3 us -> 50.1 us  [per_device(): totals = lax.psum(totals, over)]
    psum x1, blocking collectives: 39.9 us -> 24.9 us  [per_device(): totals = lax.psum(totals, over)]
  transfers between devices with their start and end apart: 9 -> 10, of which waited for: 8 -> 9; matrix products, arithmetic and copies ran while one was open for 18% -> 20% of each run, Pallas kernels for 0% -> 0%
where the time goes in v1:
time: 662 us; the launch traced here: 653 us
  waiting for transfers between devices  339 us (51%)
  blocking collectives  99.5 us (15%)
  matrix products  86.3 us (13%)
  local copies, waits for them, and re-layouts  60.2 us (9%)
  other arithmetic  42.8 us (6%)
  between operations  15.1 us (2%)
  starting transfers between devices  9.64 us (1%)
    all_gather x2, waiting for transfers between devices, gather_channels(): return lax.all_gather(values, 'tp', axis=1, tiled=True)  167 us
    reduce_scatter x2, waiting for transfers between devices, sum_channels(): lax.psum_scatter(values.astype(jnp.bfloat16), 'tp', scatter_dimension=1,...  94.7 us
    psum x2, waiting for transfers between devices, per_device(): totals = lax.psum(totals, over)  50.1 us
    psum x2, blocking collectives, norm_stats(): totals = lax.psum((jnp.sum(values, -1), jnp.sum(values * values, -1)), 'tp')  37.4 us
    psum x2, blocking collectives, norm_back(): lax.psum((jnp.sum(grad_hat, -1), jnp.sum(grad_hat * normed, -1)), 'tp')  37.1 us
    psum x1, blocking collectives, per_device(): totals = lax.psum(totals, over)  24.9 us
    dot_general x1, matrix products, per_device(): jnp.dot(grad_full, lower_rows.T, preferred_element_type=f32)  15.2 us
    all_gather x1, waiting for transfers between devices, per_device(): lax.all_gather(ch_w2.astype(bf16), 'dp', axis=1, tiled=True)  14.6 us
  transfers between devices with their start and end apart: 10, of which 9 were waited for; matrix products, arithmetic and copies ran while one was open for 20% of the time, Pallas kernels for 0%

profile of v1, /device:TPU:0, one launch (start us, length us, event | category | flops | bytes accessed | tf_op | source)
XLA Modules:
  0.0 652.9 jit_solution(9838611191693056481)
XLA Ops:
  16.1 21.5 %all-reduce.5 = (f32[16,196]{1,0:T(8,128)S(1)}, f32[16,196]{1,0:T(8,128)S(1)}) all-reduce(f32[16,196]{1,0:T(8,128)} %get-tuple-element.20, f32[16,196]{1,0:T(8,128)} %get-tuple-element.19), channel_id=1, replica_groups=mesh['dp'=8,'tp'=4] {'tp'}, use_global_device_ids=true, to_apply=%region_3.0 | all-reduce | flops 6272 | bytes 50176 | tf_op jit(solution)/shard_map/psum | solution.py:26
  46.4 15.9 %all-reduce.4 = (f32[16,196]{1,0:T(8,128)S(1)}, f32[16,196]{1,0:T(8,128)S(1)}) all-reduce(f32[16,196]{1,0:T(8,128)S(1)} %get-tuple-element.23, f32[16,196]{1,0:T(8,128)S(1)} %get-tuple-element.22), channel_id=1, replica_groups=mesh['dp'=8,'tp'=4] {'tp'}, use_global_device_ids=true, to_apply=%region_7.0 | all-reduce | flops 6272 | bytes 50176 | tf_op jit(solution)/shard_map/psum | solution.py:26
  77.1 84.4 %all-gather.5.cloned.1.call-done = bf16[3136,768]{0,1:T(8,128)(2,1)} async-done(((bf16[3136,192]{0,1:T(8,128)(2,1)}), bf16[3136,768]{0,1:T(8,128)(2,1)}) %all-gather.5.cloned.1.call-update) | async-done | bytes 4816912 | tf_op jit(solution)/shard_map/all_gather | solution.py:45
  161.5 10.4 %fusion.40 = f32[3136,768]{1,0:T(8,128)} fusion(bf16[3136,768]{0,1:T(8,128)(2,1)} %all-gather.5.cloned.1.call-done, bf16[768,768]{1,0:T(8,128)(2,1)} %all-gather.7.cloned.1.call-done), kind=kOutput, calls=%fused_computation.92 | convolution fusion | flops 3699376128 | bytes 15630336 | tf_op jit(solution)/shard_map/dot_general | solution.py:108
  171.9 14.6 %all-gather.9.cloned.1.call-done = bf16[768,768]{0,1:T(8,128)(2,1)} async-done(((bf16[768,96]{0,1:T(8,128)(2,1)}), bf16[768,768]{0,1:T(8,128)(2,1)}) %all-gather.9.cloned.1.call-update) | async-done | bytes 1179664 | tf_op jit(solution)/shard_map/all_gather | solution.py:102
  186.5 10.6 %convolution_convert_fusion.1 = bf16[3136,768]{0,1:T(8,128)(2,1)} fusion(bf16[768,768]{0,1:T(8,128)(2,1)} %all-gather.9.cloned.1.call-done, f32[3136,768]{1,0:T(8,128)} %fusion.40, f32[768]{0:T(1024)S(1)} %dynamic_slice.12), kind=kOutput, calls=%fused_computation.14 | convolution fusion | flops 3725869056 | bytes 15633408 | tf_op jit(solution)/shard_map/dot_general | solution.py:112
  197.6 83.0 %all-gather.11.cloned.1.call-done = bf16[3136,768]{0,1:T(8,128)(2,1)} async-done(((bf16[3136,192]{0,1:T(8,128)(2,1)}), bf16[3136,768]{0,1:T(8,128)(2,1)}) %all-gather.11.cloned.1.call-update) | async-done | bytes 4816912 | tf_op jit(solution)/shard_map/all_gather | solution.py:45
  280.6 15.2 %convert_reduce_fusion = (f32[768]{0:T(1024)S(1)}, bf16[3136,768]{1,0:T(8,128)(2,1)S(1)}) fusion(f32[3136,768]{1,0:T(8,128)} %fusion.40, f32[768]{0:T(1024)S(1)} %dynamic_slice.12, bf16[3136,768]{0,1:T(8,128)(2,1)} %all-gather.11.cloned.1.call-done, bf16[768,768]{0,1:T(8,128)(2,1)} %all-gather.9.cloned.1.call-done), kind=kOutput, calls=%fused_computation.9 | convolution fusion | flops 3754769664 | bytes 20453376 | tf_op jit(solution)/shard_map/dot_general | solution.py:116
  298.0 5.9 convolution_convert_fusion
  303.9 10.6 %convolution_convert_fusion.2 = bf16[768,768]{0,1:T(8,128)(2,1)} fusion(bf16[3136,768]{0,1:T(8,128)(2,1)} %all-gather.11.cloned.1.call-done, f32[3136,768]{1,0:T(8,128)} %fusion.40, f32[768]{0:T(1024)S(1)} %dynamic_slice.12), kind=kOutput, calls=%fused_computation.49 | convolution fusion | flops 3724050432 | bytes 15633408 | tf_op jit(solution)/shard_map/dot_general | solution.py:117
  318.9 9.1 %convolution_convert_fusion.3 = bf16[768,768]{1,0:T(8,128)(2,1)} fusion(bf16[3136,768]{0,1:T(8,128)(2,1)} %all-gather.5.cloned.1.call-done, bf16[3136,768]{1,0:T(8,128)(2,1)} %copy-done.29), kind=kOutput, calls=%fused_computation.50 | convolution fusion | flops 3699965952 | bytes 10813440 | tf_op jit(solution)/shard_map/dot_general | solution.py:119
  328.0 7.7 %all-to-all-done.1 = bf16[8,768,96]{1,2,0:T(8,128)(2,1)} async-done(((bf16[8,768,96]{1,2,0:T(8,128)(2,1)}), bf16[8,768,96]{1,2,0:T(8,128)(2,1)}, u32[]{:S(2)}, u32[]{:S(2)}) %all-to-all-start.1) | async-done | bytes 1179680 | tf_op jit(solution)/shard_map/all_to_all | solution.py:21
  359.0 10.6 %reduce-scatter.3.cloned.1.call-done = bf16[3136,192]{0,1:T(8,128)(2,1)} async-done(((bf16[3136,768]{0,1:T(8,128)(2,1)}), bf16[3136,192]{0,1:T(8,128)(2,1)}) %reduce-scatter.3.cloned.1.call-update) | async-done | bytes 1204240 | tf_op jit(solution)/shard_map/reduce_scatter | solution.py:49
  371.2 5.7 reshape.138
  376.9 84.1 %reduce-scatter.5.cloned.1.call-done = bf16[3136,192]{0,1:T(8,128)(2,1)} async-done(((bf16[3136,768]{0,1:T(8,128)(2,1)}), bf16[3136,192]{0,1:T(8,128)(2,1)}) %reduce-scatter.5.cloned.1.call-update) | async-done | bytes 1204240 | tf_op jit(solution)/shard_map/reduce_scatter | solution.py:49
  462.7 5.8 reshape.130
  473.8 18.5 %all-reduce.3 = (f32[16,196]{1,0:T(8,128)S(1)}, f32[16,196]{1,0:T(8,128)S(1)}) all-reduce(f32[16,196]{1,0:T(8,128)S(1)} %get-tuple-element.18, f32[16,196]{1,0:T(8,128)S(1)} %reduce_sum.187), channel_id=1, replica_groups=mesh['dp'=8,'tp'=4] {'tp'}, use_global_device_ids=true, to_apply=%region_13.0 | all-reduce | flops 6272 | bytes 50176 | tf_op jit(solution)/shard_map/psum | solution.py:33
  492.4 8.5 %convert_reduce_fusion.3 = (f32[196]{0:T(256)}, f32[16,196,192]{1,2,0:T(8,128)S(1)}, bf16[16,196,192]{1,2,0:T(8,128)(2,1)}) fusion(f32[16,196,192]{1,2,0:T(8,128)} %copy.76, f32[16,196]{1,0:T(8,128)S(1)} %get-tuple-element.39, f32[16,196,192]{1,2,0:T(8,128)} %copy-done.2, f32[16,196]{1,0:T(8,128)S(1)} %get-tuple-element.55, ...), kind=kLoop, calls=%fused_computation.32 | loop fusion | flops 8429372 | bytes 13298192 | tf_op jit(solution)/shard_map/reduce_sum | solution.py:139
  500.9 6.2 convolution_bitcast_fusion
  507.1 5.5 convert_reduce_fusion.1
  534.5 18.6 %all-reduce.2 = (f32[16,196]{1,0:T(8,128)S(1)}, f32[16,196]{1,0:T(8,128)S(1)}, f32[2,768]{1,0:T(2,128)S(1)}, f32[384]{0:T(512)S(1)}, f32[196]{0:T(256)S(1)}, /*index=5*/f32[3072]{0:T(1024)S(1)}, f32[768]{0:T(1024)S(1)}) all-reduce(f32[16,196]{1,0:T(8,128)S(1)} %get-tuple-element.16, ...), channel_id=1, replica_groups=mesh['dp'=8,'tp'=4] {'tp'}, use_global_device_ids=true, to_apply=%region_17.0 | all-reduce | flops 12228 | bytes 97824 | tf_op jit(solution)/shard_map/psum | solution.py:33
  553.2 25.5 %all-reduce.12.cloned.1.call-done = (f32[64,2,768]{2,0,1:T(8,128)}, f32[196,384]{1,0:T(8,128)}, f32[384,196]{0,1:T(8,128)}) async-done(((f32[64,2,768]{2,0,1:T(8,128)}, f32[196,384]{1,0:T(8,128)}, f32[384,196]{0,1:T(8,128)}), (f32[64,2,768]{2,0,1:T(8,128)}, f32[196,384]{1,0:T(8,128)}, f32[384,196]{0,1:T(8,128)})) %all-reduce.12.cloned.1.call-update) | async-done | bytes 995344 | tf_op jit(solution)/shard_map/psum | solution.py:164
  589.2 24.9 %all-reduce = (f32[2,768]{1,0:T(2,128)S(1)}, f32[384]{0:T(512)}, f32[196]{0:T(256)}, f32[3072]{0:T(1024)}, f32[768]{0:T(1024)}) all-reduce(f32[2,768]{1,0:T(2,128)S(1)} %get-tuple-element.34, f32[384]{0:T(512)S(1)} %get-tuple-element.35, f32[196]{0:T(256)S(1)} %get-tuple-element.36, ...), channel_id=1, replica_groups=mesh['dp'=8,'tp'=4] {'dp'}, use_global_device_ids=true, to_apply=%region_26.0 | all-reduce | flops 5956 | bytes 47648 | tf_op jit(solution)/shard_map/psum | solution.py:164
  614.2 24.6 %all-reduce.10.cloned.1.call-done = (f32[64,2,768]{2,0,1:T(8,128)}, f32[196,384]{1,0:T(8,128)}, f32[384,196]{0,1:T(8,128)}) async-done(((f32[64,2,768]{2,0,1:T(8,128)}, f32[196,384]{1,0:T(8,128)}, f32[384,196]{0,1:T(8,128)}), (f32[64,2,768]{2,0,1:T(8,128)}, f32[196,384]{1,0:T(8,128)}, f32[384,196]{0,1:T(8,128)})) %all-reduce.10.cloned.1.call-update) | async-done | bytes 995344 | tf_op jit(solution)/shard_map/psum | solution.py:164
  (149 shorter events, 110.3 us)
Async XLA Ops:
  7.2 69.9 %all-gather.7.cloned.1.call-start = ((), (), s32[]{:S(2)}) async-start(), calls=%async_computation.5 | async-start | bytes 1327104 | tf_op jit(solution)/shard_map/all_gather | solution.py:101
  8.9 152.6 %all-gather.5.cloned.1.call-start = ((), (), s32[]{:S(2)}) async-start(), calls=%async_computation.4 | async-start | bytes 6144000 | tf_op jit(solution)/shard_map/all_gather | solution.py:45
  12.9 25.4 %copy-start.16 = (f32[192]{0:T(256)S(1)}, f32[192]{0:T(256)}, u32[]{:S(2)}) copy-start(f32[192]{0:T(256)} %param.16) | copy-start | bytes 2308
  16.1 25.8 %copy-start.7 = (f32[196,384]{1,0:T(8,128)S(1)}, f32[196,384]{1,0:T(8,128)}, u32[]{:S(2)}) copy-start(f32[196,384]{1,0:T(8,128)} %param.18) | copy-start | bytes 903172
  43.9 18.4 %copy-start.15 = (f32[192]{0:T(256)S(1)}, f32[192]{0:T(256)}, u32[]{:S(2)}) copy-start(f32[192]{0:T(256)} %param.22) | copy-start | bytes 2308
  43.9 18.4 %copy-start.21 = (f32[192]{0:T(256)S(1)}, f32[192]{0:T(256)}, u32[]{:S(2)}) copy-start(f32[192]{0:T(256)} %param.23) | copy-start | bytes 2308
  46.4 18.5 %copy-start.2 = (f32[16,196,192]{1,2,0:T(8,128)}, f32[16,196,192]{1,2,0:T(8,128)S(1)}, u32[]{:S(2)}) copy-start(f32[16,196,192]{1,2,0:T(8,128)S(1)} %get-tuple-element.63) | copy-start | bytes 7225348
  69.3 117.2 %all-gather.9.cloned.1.call-start = ((), (), s32[]{:S(2)}) async-start(), calls=%async_computation.6 | async-start | bytes 1327104 | tf_op jit(solution)/shard_map/all_gather | solution.py:102
  71.0 209.6 %all-gather.11.cloned.1.call-start = ((), (), s32[]{:S(2)}) async-start(), calls=%async_computation.8 | async-start | bytes 6144000 | tf_op jit(solution)/shard_map/all_gather | solution.py:45
  76.1 293.6 %reduce-scatter.3.cloned.1.call-start = ((), (), s32[]{:S(2)}) async-start(), calls=%async_computation.7 | async-start | bytes 6144000 | tf_op jit(solution)/shard_map/reduce_scatter | solution.py:49
  197.1 100.9 %copy-start.23 = (bf16[768,768]{1,0:T(8,128)(2,1)S(1)}, bf16[768,768]{1,0:T(8,128)(2,1)}, u32[]{:S(2)}) copy-start(bf16[768,768]{1,0:T(8,128)(2,1)} %all-gather.7.cloned.1.call-done) | copy-start | bytes 3538948
  197.1 263.8 %reduce-scatter.5.cloned.1.call-start = ((), (), s32[]{:S(2)}) async-start(), calls=%async_computation.9 | async-start | bytes 6144000 | tf_op jit(solution)/shard_map/reduce_scatter | solution.py:49
  314.5 21.3 %all-to-all-start.1 = ((bf16[8,768,96]{1,2,0:T(8,128)(2,1)}), bf16[8,768,96]{1,2,0:T(8,128)(2,1)}, u32[]{:S(2)}, u32[]{:S(2)}) async-start(bf16[8,768,96]{1,2,0:T(8,128)(2,1)} %bitcast.18), calls=%async_computation.3 | async-start | bytes 2359296 | tf_op jit(solution)/shard_map/all_to_all | solution.py:21
  328.0 12.1 %copy-start.5 = (bf16[16,1,37632]{2,0,1:T(8,128)(2,1)S(1)}, bf16[16,1,37632]{2,0,1:T(8,128)(2,1)}, u32[]{:S(2)}) copy-start(bf16[16,1,37632]{2,0,1:T(8,128)(2,1)} %param.29) | copy-start | bytes 3612676
  335.8 21.1 %all-to-all-start = ((bf16[8,96,768]{2,1,0:T(8,128)(2,1)}), bf16[8,96,768]{2,1,0:T(8,128)(2,1)}, u32[]{:S(2)}, u32[]{:S(2)}) async-start(bf16[8,96,768]{2,1,0:T(8,128)(2,1)} %bitcast.81), calls=%async_computation.2 | async-start | bytes 2359296 | tf_op jit(solution)/shard_map/all_to_all | solution.py:21
  340.0 238.6 %all-reduce.12.cloned.1.call-start = ((), (), s32[]{:S(2)}) async-start(), calls=%async_computation.11 | async-start | bytes 2015232 | tf_op jit(solution)/shard_map/psum | solution.py:164
  492.3 8.6 %copy-start.27 = (f32[384]{0:T(512)S(1)}, f32[384]{0:T(512)}, u32[]{:S(2)}) copy-start(f32[384]{0:T(512)} %param.19) | copy-start | bytes 4612
  492.4 14.7 %slice-start = ((s8[4718592]{0:T(1024)(128)(4,1)}), s8[4194304]{0:T(1024)(128)(4,1)S(1)}, s32[]{:S(2)}) async-start(s8[4718592]{0:T(1024)(128)(4,1)} %bitcast.79), calls=%async_computation.12 | async-start | bytes 8388608
  519.4 7.4 %copy-start.1 = (f32[16,196,192]{1,2,0:T(8,128)S(1)}, f32[16,196,192]{1,2,0:T(8,128)}, u32[]{:S(2)}) copy-start(f32[16,196,192]{1,2,0:T(8,128)} %copy.70) | copy-start | bytes 7225348
  519.4 7.4 %copy-start.9 = (f32[16,196]{1,0:T(8,128)S(1)}, f32[16,196]{1,0:T(8,128)}, u32[]{:S(2)}) copy-start(f32[16,196]{1,0:T(8,128)} %copy-done.8) | copy-start | bytes 37636
  519.4 7.4 %copy-start.11 = (f32[16,196]{1,0:T(8,128)S(1)}, f32[16,196]{1,0:T(8,128)}, u32[]{:S(2)}) copy-start(f32[16,196]{1,0:T(8,128)} %copy-done.10) | copy-start | bytes 37636
  519.4 7.4 %copy-start.17 = (f32[192]{0:T(256)S(1)}, f32[192]{0:T(256)}, u32[]{:S(2)}) copy-start(f32[192]{0:T(256)} %param.16) | copy-start | bytes 2308
  526.7 112.1 %all-reduce.10.cloned.1.call-start = ((), (), s32[]{:S(2)}) async-start(), calls=%async_computation.10 | async-start | bytes 2015232 | tf_op jit(solution)/shard_map/psum | solution.py:164
  532.1 46.5 %copy-start.18 = (f32[192]{0:T(256)S(1)}, f32[192]{0:T(256)}, u32[]{:S(2)}) copy-start(f32[192]{0:T(256)} %param.16) | copy-start | bytes 2308
  (18 other events, 52.2 us)
Sparse Core Ops, SparseCore 0:
  10.5 26.7 all-gather.6
  69.4 92.0 all-gather.4
  164.0 22.4 all-gather.8
  187.9 92.6 all-gather.10
  282.8 86.8 reduce-scatter.2
  372.0 88.9 reduce-scatter.4
  526.8 51.7 all-reduce.11
  582.6 56.2 all-reduce.9
